TPU v7x, 256 devices: a whole 4x4x8 slice. The times are simulated.
256 devices in a mesh: seq: 32 (over z, y_lo, core), chan: 8 (over y_hi, x).
Axes of the slice: x: 4, y: 4 (y_hi: 2, y_lo: 2; y = y_hi * 2 + y_lo), z: 8, core: 2. Of those that a mesh axis runs over, the one named last changes fastest.
Arguments:
- projected: bfloat16 [8192, 3, 4096], P('seq', None, 'chan'), may hold values from -6 to 6
- short_weight: float32 [3, 3, 4096], P(None, None, 'chan'), may hold values from -3 to 3
- filters: float32 [512, 8192], P(('chan', 'seq')), may hold values from -1.1 to 1.1
- skip: float32 [4096], P('chan'), may hold values from -3 to 3
- out_weight: bfloat16 [4096, 4096], P('chan', 'seq'), may hold values from -0.09375 to 0.09375
- cotangent: bfloat16 [8192, 4096], P('seq', 'chan'), may hold values from -6 to 6
Outputs:
- mixed: bfloat16 [8192, 4096], P('seq', 'chan')
- projected_grad: bfloat16 [8192, 3, 4096], P('seq', None, 'chan')
- filter_grad: float32 [512, 8192], P(('chan', 'seq'))
All inputs are finite; a program needn't handle non-finite values.
Results may differ from a plain program's by a relative error of at most 0.008.
Values may be sent and summed in bfloat16 or wider, within the bound.
No kernel may reach another device: no remote copies, remote signals or barrier semaphores. Data moves between devices by JAX's collectives and lax.ppermute only.
A program may use at most 64 MiB of HBM per device.

v0:
```python
import math
import jax
import jax.numpy as jnp
from jax import lax
from jax.sharding import PartitionSpec as P

GROUP = 8
SHORT = 3
FFT_ROWS = 128
exact_mode = lax.Precision.HIGHEST


def from_behind(shard, axis, by):
    count = lax.axis_size(axis)
    pairs = [(i, i + by) for i in range(count) if 0 <= i + by < count]
    return lax.ppermute(shard, axis, pairs)


def fourier_tables(rows_count, cols_count):
    total = rows_count * cols_count
    freq_rows = jnp.arange(rows_count, dtype=jnp.int32)
    half_rows = jnp.arange(rows_count // 2, dtype=jnp.int32)
    freq_cols = jnp.arange(cols_count, dtype=jnp.int32)
    turn = 2.0 * math.pi
    angle_first = (
        turn
        * (freq_rows[:, None] * half_rows[None, :] % rows_count).astype(jnp.float32)
        / rows_count
    )
    angle_second = (
        turn
        * (freq_cols[:, None] * freq_cols[None, :] % cols_count).astype(jnp.float32)
        / cols_count
    )
    angle_twist = (
        turn * (freq_rows[:, None] * freq_cols[None, :] % total).astype(jnp.float32) / total
    )
    return (
        jnp.cos(angle_first),
        jnp.sin(angle_first),
        jnp.cos(angle_second),
        jnp.sin(angle_second),
        jnp.cos(angle_twist),
        jnp.sin(angle_twist),
    )


def split_product(table, folded):
    table_high = table.astype(jnp.bfloat16)
    table_low = (table - table_high.astype(jnp.float32)).astype(jnp.bfloat16)
    return jnp.einsum(
        "kn,cnm->ckm", table_high, folded, preferred_element_type=jnp.float32
    ) + jnp.einsum("kn,cnm->ckm", table_low, folded, preferred_element_type=jnp.float32)


def forward_spectrum(signal, tables):
    cos_first, sin_first, cos_second, sin_second, cos_twist, sin_twist = tables
    count = signal.shape[0]
    folded = signal.reshape(count, cos_first.shape[1], cos_second.shape[0])
    if signal.dtype == jnp.bfloat16:
        first_re = split_product(cos_first, folded)
        first_im = -split_product(sin_first, folded)
    else:
        first_re = jnp.einsum("kn,cnm->ckm", cos_first, folded, precision=exact_mode)
        first_im = -jnp.einsum("kn,cnm->ckm", sin_first, folded, precision=exact_mode)
    turned_re = first_re * cos_twist + first_im * sin_twist
    turned_im = first_im * cos_twist - first_re * sin_twist
    spec_re = jnp.einsum("ckn,nm->ckm", turned_re, cos_second, precision=exact_mode) + jnp.einsum(
        "ckn,nm->ckm", turned_im, sin_second, precision=exact_mode
    )
    spec_im = jnp.einsum("ckn,nm->ckm", turned_im, cos_second, precision=exact_mode) - jnp.einsum(
        "ckn,nm->ckm", turned_re, sin_second, precision=exact_mode
    )
    return (spec_re, spec_im)


def inverse_signal(spec_re, spec_im, tables):
    cos_first, sin_first, cos_second, sin_second, cos_twist, sin_twist = tables
    count = spec_re.shape[0]
    total = cos_first.shape[0] * cos_second.shape[0]
    inner_re = jnp.einsum("ckm,mn->ckn", spec_re, cos_second, precision=exact_mode) - jnp.einsum(
        "ckm,mn->ckn", spec_im, sin_second, precision=exact_mode
    )
    inner_im = jnp.einsum("ckm,mn->ckn", spec_im, cos_second, precision=exact_mode) + jnp.einsum(
        "ckm,mn->ckn", spec_re, sin_second, precision=exact_mode
    )
    turned_re = inner_re * cos_twist - inner_im * sin_twist
    turned_im = inner_im * cos_twist + inner_re * sin_twist
    signal = jnp.einsum("kn,ckm->cnm", cos_first, turned_re, precision=exact_mode) - jnp.einsum(
        "kn,ckm->cnm", sin_first, turned_im, precision=exact_mode
    )
    return (signal / total).reshape(count, -1)


def grouped(spectrum, groups_dev):
    return spectrum.reshape(groups_dev, GROUP, spectrum.shape[1], spectrum.shape[2])


def channel_major(block):
    return lax.all_to_all(block, "seq", split_axis=0, concat_axis=1, tiled=True)


def token_major(block):
    return lax.all_to_all(block, "seq", split_axis=1, concat_axis=0, tiled=True)


def on_device(projected, short_weight, filters, skip, out_weight, cotangent):
    tok_rows = projected.shape[0]
    groups_dev = filters.shape[0]
    seq_length = filters.shape[1]
    rim = SHORT - 1
    tables = fourier_tables(FFT_ROWS, 2 * seq_length // FFT_ROWS)
    before = from_behind(projected[tok_rows - rim :], "seq", 1)
    extended = jnp.concatenate([before, projected], axis=0).astype(jnp.float32)
    short = short_weight[:, 0, :] * extended[0:tok_rows]
    for j in range(1, SHORT):
        short = short + short_weight[:, j, :] * extended[j : j + tok_rows]
    query_side = short[:, 0]
    key_side = short[:, 1]
    value_side = short[:, 2]
    carried = (key_side * value_side).astype(jnp.bfloat16)
    carried_seq = channel_major(carried.T)
    kept_re, kept_im = forward_spectrum(carried_seq, tables)
    filt_re, filt_im = forward_spectrum(filters, tables)
    group_re = grouped(kept_re, groups_dev)
    group_im = grouped(kept_im, groups_dev)
    conv_re = (group_re * filt_re[:, None] - group_im * filt_im[:, None]).reshape(kept_re.shape)
    conv_im = (group_re * filt_im[:, None] + group_im * filt_re[:, None]).reshape(kept_re.shape)
    conv_seq = inverse_signal(conv_re, conv_im, tables).astype(jnp.bfloat16)
    conv = token_major(conv_seq).T
    mixed_in = conv.astype(jnp.float32) + skip * carried.astype(jnp.float32)
    gated = (query_side * mixed_in).astype(jnp.bfloat16)
    weight_rows = lax.all_gather(out_weight, "seq", axis=1, tiled=True)
    mixed = lax.psum_scatter(
        lax.dot_general(
            weight_rows, gated, (((0,), (1,)), ((), ())), preferred_element_type=jnp.float32
        ),
        "chan",
        scatter_dimension=0,
        tiled=True,
    ).T.astype(jnp.bfloat16)
    grad_full = lax.all_gather(cotangent, "chan", axis=1, tiled=True)
    gated_grad = lax.dot_general(
        grad_full, weight_rows, (((1,), (1,)), ((), ())), preferred_element_type=jnp.float32
    )
    query_grad = gated_grad * mixed_in
    mixed_grad = (gated_grad * query_side).astype(jnp.bfloat16)
    grad_seq = channel_major(mixed_grad.T)
    grad_re, grad_im = forward_spectrum(grad_seq, tables)
    ggrad_re = grouped(grad_re, groups_dev)
    ggrad_im = grouped(grad_im, groups_dev)
    back_re = (ggrad_re * filt_re[:, None] + ggrad_im * filt_im[:, None]).reshape(grad_re.shape)
    back_im = (ggrad_im * filt_re[:, None] - ggrad_re * filt_im[:, None]).reshape(grad_re.shape)
    back_seq = inverse_signal(back_re, back_im, tables).astype(jnp.bfloat16)
    back = token_major(back_seq).T
    cross_re = jnp.sum(ggrad_re * group_re + ggrad_im * group_im, axis=1)
    cross_im = jnp.sum(ggrad_im * group_re - ggrad_re * group_im, axis=1)
    filter_grad = inverse_signal(cross_re, cross_im, tables) * (1.0 / math.sqrt(GROUP * seq_length))
    carried_grad = back.astype(jnp.float32) + skip * mixed_grad.astype(jnp.float32)
    short_grad = jnp.stack([query_grad, carried_grad * value_side, carried_grad * key_side], axis=1)
    after = from_behind(short_grad[:rim], "seq", -1)
    extended_grad = jnp.concatenate([short_grad, after], axis=0)
    projected_grad = short_weight[:, 0, :] * extended_grad[rim : rim + tok_rows]
    for j in range(1, SHORT):
        projected_grad = (
            projected_grad + short_weight[:, j, :] * extended_grad[rim - j : rim - j + tok_rows]
        )
    return (mixed, projected_grad.astype(jnp.bfloat16), filter_grad)


def solution(mesh):
    placed = (
        P("seq", None, "chan"),
        P(None, None, "chan"),
        P(("chan", "seq"), None),
        P("chan"),
        P("chan", "seq"),
        P("seq", "chan"),
    )
    return jax.shard_map(
        on_device,
        mesh=mesh,
        in_specs=placed,
        out_specs=(P("seq", "chan"), P("seq", None, "chan"), P(("chan", "seq"), None)),
        check_vma=False,
    )
```

profile of v0, /device:TPU:2, one launch (start us, length us, event | category | flops | bytes accessed | tf_op | source)
XLA Modules:
  0.0 367.4 jit_solution(16333220502571178986)
XLA Ops:
  7.2 0.7 all-gather.5.cloned.1.call-update
  8.0 0.7 all-gather.3.cloned.1.call-update
  8.7 0.7 slice.43
  9.4 1.7 collective-permute-start
  11.5 0.9 fusion.347
  12.3 1.3 convolution_negate_fusion
  13.6 1.3 fusion.68
  14.9 0.5 fusion.50
  15.7 0.5 fusion.3
  16.2 59.0 %all-gather.5.cloned.1.call-done = bf16[256,4096]{1,0:T(8,128)(2,1)} async-done(((bf16[256,512]{1,0:T(8,128)(2,1)}), bf16[256,4096]{1,0:T(8,128)(2,1)}) %all-gather.5.cloned.1.call-update) | async-done | bytes 2097168 | tf_op jit(solution)/shard_map/all_gather | solution.py:142
  75.2 73.1 %all-gather.3.cloned.1.call-done = bf16[512,4096]{1,0:T(8,128)(2,1)} async-done(((bf16[512,128]{1,0:T(8,128)(2,1)}), bf16[512,4096]{1,0:T(8,128)(2,1)}) %all-gather.3.cloned.1.call-update) | async-done | bytes 4194320 | tf_op jit(solution)/shard_map/all_gather | solution.py:133
  148.3 4.9 %multiply_convert_fusion = (bf16[256,512]{1,0:T(8,128)(2,1)S(1)}, f32[256,512]{1,0:T(8,128)}) fusion(f32[256,3,512]{2,0,1:T(8,128)S(1)} %fusion.3, bf16[256,4096]{1,0:T(8,128)(2,1)} %all-gather.5.cloned.1.call-done, bf16[512,4096]{1,0:T(8,128)(2,1)} %all-gather.3.cloned.1.call-done), kind=kOutput, calls=%fused_computation.89 | convolution fusion | flops 1074003968 | bytes 7602176 | tf_op jit(solution)/shard_map/dot_general | solution.py:143
  153.2 0.8 copy.51
  154.0 5.3 %all-to-all-start.2 = ((bf16[32,16,256]{2,1,0:T(8,128)(2,1)}), bf16[32,16,256]{2,1,0:T(8,128)(2,1)S(1)}, u32[]{:S(2)}, u32[]{:S(2)}) async-start(bf16[32,16,256]{2,1,0:T(8,128)(2,1)} %bitcast.28), calls=%async_computation.3 | async-start | bytes 524288 | tf_op jit(solution)/shard_map/all_to_all | solution.py:100
  159.5 0.5 fusion.54
  160.2 0.5 convolution_subtract_fusion.7
  160.8 0.5 convolution_add_fusion.9
  161.3 10.3 %all-to-all-done.2 = bf16[32,16,256]{2,1,0:T(8,128)(2,1)S(1)} async-done(((bf16[32,16,256]{2,1,0:T(8,128)(2,1)}), bf16[32,16,256]{2,1,0:T(8,128)(2,1)S(1)}, u32[]{:S(2)}, u32[]{:S(2)}) %all-to-all-start.2) | async-done | bytes 262176 | tf_op jit(solution)/shard_map/all_to_all | solution.py:100
  172.3 0.4 fusion.161
  172.7 0.4 fusion.6
  173.1 0.4 fusion.7
  173.6 2.1 fusion.48
  175.6 2.1 fusion.47
  177.7 2.1 convolution_subtract_fusion.1
  179.8 3.1 fusion.21
  182.9 1.6 fusion.88
  184.5 1.3 fusion.86
  185.8 1.4 convolution_subtract_fusion
  187.2 1.3 convolution_add_fusion
  188.6 1.5 fusion.26
  190.1 1.5 fusion.15
  191.8 15.3 %all_to_all.52 = bf16[16,32,256]{2,0,1:T(8,128)(2,1)S(1)} all-to-all(bf16[16,32,256]{2,0,1:T(8,128)(2,1)S(1)} %copy.63), channel_id=1, replica_groups=mesh['seq'=32,'chan'=8] {'seq'}, dimensions={1} | all-to-all | bytes 524288 | tf_op jit(solution)/shard_map/all_to_all | solution.py:104
  207.5 1.4 multiply_bitcast_fusion.1
  209.0 15.4 %all_to_all.53 = bf16[32,16,256]{2,1,0:T(8,128)(2,1)S(1)} all-to-all(bf16[32,16,256]{2,1,0:T(8,128)(2,1)S(1)} %bitcast.243), channel_id=1, replica_groups=mesh['seq'=32,'chan'=8] {'seq'}, dimensions={0} | all-to-all | bytes 524288 | tf_op jit(solution)/shard_map/all_to_all | solution.py:100
  225.0 0.4 fusion.163
  225.4 0.4 fusion.9
  225.9 0.4 fusion.10
  226.3 2.1 fusion.46
  228.4 2.1 fusion.45
  230.5 2.1 convolution_subtract_fusion.3
  232.6 3.1 fusion.19
  235.7 1.3 fusion.94
  237.0 1.5 fusion.92
  238.6 1.4 convolution_subtract_fusion.2
  239.9 1.3 convolution_add_fusion.2
  241.3 1.5 fusion.33
  242.8 2.2 fusion.16
  245.0 1.7 convert_element_type.266
  246.7 1.1 copy.49
  247.8 15.4 %all_to_all.54 = bf16[16,32,256]{2,0,1:T(8,128)(2,1)S(1)} all-to-all(bf16[16,32,256]{2,0,1:T(8,128)(2,1)S(1)} %copy.49), channel_id=1, replica_groups=mesh['seq'=32,'chan'=8] {'seq'}, dimensions={1} | all-to-all | bytes 524288 | tf_op jit(solution)/shard_map/all_to_all | solution.py:104
  263.2 0.9 convert_element_type.289
  264.1 2.1 copy.50
  266.1 5.8 %convolution_bitcast_fusion = f32[4096,256]{0,1:T(8,128)} fusion(bf16[512,4096]{1,0:T(8,128)(2,1)} %all-gather.3.cloned.1.call-done, f32[256,3,512]{2,0,1:T(8,128)} %copy-done, bf16[256,512]{1,0:T(8,128)(2,1)S(1)} %get-tuple-element.11, f32[512,256]{0,1:T(8,128)} %copy.50, f32[512]{0:T(512)S(1)} %copy-done.15), kind=kOutput, calls=%fused_computation | convolution fusion | flops 1074397184 | bytes 9701376 | tf_op jit(solution)/shard_map/dot_general | solution.py:135
  272.0 2.1 bitcast_reduce_fusion.1
  274.1 0.5 fusion.84
  274.6 0.5 fusion.82
  275.1 0.5 convolution_subtract_fusion.6
  275.6 0.5 convolution_add_fusion.8
  276.8 1.3 collective-permute-start.1
  278.5 0.7 copy.102
  279.2 0.7 collective-permute-done.1
  280.1 1.4 fusion.2
  281.5 77.4 %reduce-scatter.2.cloned.1.call-done = f32[512,256]{0,1:T(8,128)} async-done(((f32[4096,256]{0,1:T(8,128)}), f32[512,256]{0,1:T(8,128)}) %reduce-scatter.2.cloned.1.call-update) | async-done | bytes 524304 | tf_op jit(solution)/shard_map/reduce_scatter | solution.py:134
  358.9 1.8 convert_bitcast_fusion
  (62 shorter events, 4.0 us)
Async XLA Ops:
  7.2 8.3 %copy-start.10 = (bf16[256,3,512]{2,0,1:T(8,128)(2,1)S(1)}, bf16[256,3,512]{2,0,1:T(8,128)(2,1)}, u32[]{:S(2)}) copy-start(bf16[256,3,512]{2,0,1:T(8,128)(2,1)} %param.6) | copy-start | bytes 2359300
  7.2 68.0 %all-gather.5.cloned.1.call-start = ((), (), s32[]{:S(2)}) async-start(), calls=%async_computation.7 | async-start | bytes 2359296 | tf_op jit(solution)/shard_map/all_gather | solution.py:142
  7.9 140.4 %all-gather.3.cloned.1.call-start = ((), (), s32[]{:S(2)}) async-start(), calls=%async_computation.5 | async-start | bytes 4325376 | tf_op jit(solution)/shard_map/all_gather | solution.py:133
  9.4 6.1 %collective-permute-start = (bf16[2,3,512]{2,0,1:T(2,128)(2,1)S(1)}, bf16[2,3,512]{2,0,1:T(2,128)(2,1)S(1)}, u32[]{:S(2)}, u32[]{:S(2)}) collective-permute-start(bf16[2,3,512]{2,0,1:T(2,128)(2,1)S(1)} %slice.43), channel_id=1, source_target_pairs={{0,8},{8,16},{16,24},{24,32},{32,40},{40,48},{48,56},{56,64},{64,7... | collective-permute-start | bytes 18440 | tf_op jit(solution)/shard_map/ppermute | solution.py:16
  11.4 149.3 %copy-start.2 = (f32[128,128]{1,0:T(8,128)}, f32[128,128]{1,0:T(8,128)S(1)}, u32[]{:S(2)}) copy-start(f32[128,128]{1,0:T(8,128)S(1)} %get-tuple-element.21) | copy-start | bytes 196612
  11.4 149.3 %copy-start.4 = (f32[128,128]{1,0:T(8,128)}, f32[128,128]{1,0:T(8,128)S(1)}, u32[]{:S(2)}) copy-start(f32[128,128]{1,0:T(8,128)S(1)} %get-tuple-element.22) | copy-start | bytes 196612
  15.5 0.7 copy-start.12
  16.2 137.0 %copy-start = (f32[256,3,512]{2,0,1:T(8,128)}, f32[256,3,512]{2,0,1:T(8,128)S(1)}, u32[]{:S(2)}) copy-start(f32[256,3,512]{2,0,1:T(8,128)S(1)} %fusion.3) | copy-start | bytes 4718596
  154.0 17.7 %all-to-all-start.2 = ((bf16[32,16,256]{2,1,0:T(8,128)(2,1)}), bf16[32,16,256]{2,1,0:T(8,128)(2,1)S(1)}, u32[]{:S(2)}, u32[]{:S(2)}) async-start(bf16[32,16,256]{2,1,0:T(8,128)(2,1)} %bitcast.28), calls=%async_computation.3 | async-start | bytes 524288 | tf_op jit(solution)/shard_map/all_to_all | solution.py:100
  159.3 199.6 %reduce-scatter.2.cloned.1.call-start = ((), (), s32[]{:S(2)}) async-start(), calls=%async_computation.6 | async-start | bytes 4718592 | tf_op jit(solution)/shard_map/reduce_scatter | solution.py:134
  160.8 19.0 %copy-start.6 = (f32[2,128,128]{2,1,0:T(8,128)}, f32[2,128,128]{2,1,0:T(8,128)S(1)}, u32[]{:S(2)}) copy-start(f32[2,128,128]{2,1,0:T(8,128)S(1)} %convolution_subtract_fusion.7) | copy-start | bytes 393220
  161.3 18.5 %copy-start.8 = (f32[2,128,128]{2,1,0:T(8,128)}, f32[2,128,128]{2,1,0:T(8,128)S(1)}, u32[]{:S(2)}) copy-start(f32[2,128,128]{2,1,0:T(8,128)S(1)} %convolution_add_fusion.9) | copy-start | bytes 393220
  191.7 15.8 %copy-start.14 = (f32[512]{0:T(512)S(1)}, f32[512]{0:T(512)}, u32[]{:S(2)}) copy-start(f32[512]{0:T(512)} %param.9) | copy-start | bytes 6148
  230.4 2.1 copy-start.7
  230.4 2.1 copy-start.9
  246.7 19.4 %copy-start.15 = (f32[512]{0:T(512)S(1)}, f32[512]{0:T(512)}, u32[]{:S(2)}) copy-start(f32[512]{0:T(512)} %param.9) | copy-start | bytes 6148
  272.0 4.2 %copy-start.3 = (f32[128,128]{1,0:T(8,128)S(1)}, f32[128,128]{1,0:T(8,128)}, u32[]{:S(2)}) copy-start(f32[128,128]{1,0:T(8,128)} %copy-done.2) | copy-start | bytes 196612
  272.0 4.2 %copy-start.5 = (f32[128,128]{1,0:T(8,128)S(1)}, f32[128,128]{1,0:T(8,128)}, u32[]{:S(2)}) copy-start(f32[128,128]{1,0:T(8,128)} %copy-done.4) | copy-start | bytes 196612
  274.1 2.5 copy-start.1
  274.1 2.5 copy-start.11
  274.1 2.5 copy-start.16
  276.8 3.1 collective-permute-start.1
  279.2 0.9 copy-start.13
Sparse Core Ops, SparseCore 0:
  10.5 64.6 all-gather.4
  76.9 71.2 all-gather.2
  272.1 86.7 reduce-scatter.1
where the time goes:
time: 372 us; the launch traced here: 367 us
  waiting for transfers between devices  222 us (60%)
  matrix products  58 us (16%)
  blocking collectives  46.1 us (12%)
  between operations  14.6 us (4%)
  local copies, waits for them, and re-layouts  9.25 us (2%)
  other arithmetic  8.93 us (2%)
  starting transfers between devices  8.58 us (2%)
    reduce_scatter x1, waiting for transfers between devices, on_device(): lax.psum_scatter(lax.dot_general(weight_rows, gated, (((0,), (1,)), ((),...  77.4 us
    all_gather x1, waiting for transfers between devices, on_device(): weight_rows = lax.all_gather(out_weight, 'seq', axis=1, tiled=True)  73.1 us
    all_gather x1, waiting for transfers between devices, on_device(): grad_full = lax.all_gather(cotangent, 'chan', axis=1, tiled=True)  59 us
    all_to_all x2, blocking collectives, token_major(): return lax.all_to_all(block, 'seq', split_axis=1, concat_axis=0, tiled=True)  30.7 us
    all_to_all x1, blocking collectives, channel_major(): return lax.all_to_all(block, 'seq', split_axis=0, concat_axis=1, tiled=True)  15.4 us
    all_to_all x1, waiting for transfers between devices, channel_major(): return lax.all_to_all(block, 'seq', split_axis=0, concat_axis=1, tiled=True)  10.3 us
  transfers between devices with their start and end apart: 6, of which 5 were waited for; matrix products, arithmetic and copies ran while one was open for 4% of the time, Pallas kernels for 0%

commit v1 on v0

--- a/solution.py
+++ b/solution.py
@@ -139,7 +139,9 @@
         scatter_dimension=0,
         tiled=True,
     ).T.astype(jnp.bfloat16)
-    grad_full = lax.all_gather(cotangent, "chan", axis=1, tiled=True)
+    grad_full = jnp.concatenate(
+        lax.all_to_all(jnp.stack([cotangent] * lax.axis_size("chan")), "chan", 0, 0), axis=1
+    )
     gated_grad = lax.dot_general(
         grad_full, weight_rows, (((1,), (1,)), ((), ())), preferred_element_type=jnp.float32
     )

time: 372 us -> 325 us (0.87)
  waiting for transfers between devices: 222 us -> 168 us
  starting transfers between devices: 8.58 us -> 15.8 us
    all_gather x1 -> x0, waiting for transfers between devices: 59 us -> none  [on_device(): grad_full = lax.all_gather(cotangent, 'chan', axis=1, tiled=True)]
    all_to_all x0 -> x1, waiting for transfers between devices: none -> 23.5 us  [on_device(): lax.all_to_all(jnp.stack([cotangent] * lax.axis_size('chan')), 'chan', 0, 0)]
    all_gather x1, waiting for transfers between devices: 73.1 us -> 55.2 us  [on_device(): weight_rows = lax.all_gather(out_weight, 'seq', axis=1, tiled=True)]
    all_to_all x0 -> x1, starting transfers between devices: none -> 7.59 us  [on_device(): lax.all_to_all(jnp.stack([cotangent] * lax.axis_size('chan')), 'chan', 0, 0)]
where the time goes in v1:
time: 325 us; the launch traced here: 320 us
  waiting for transfers between devices  168 us (52%)
  matrix products  56.3 us (17%)
  blocking collectives  46.1 us (14%)
  starting transfers between devices  15.8 us (5%)
  between operations  14.9 us (5%)
  local copies, waits for them, and re-layouts  10.3 us (3%)
  other arithmetic  8.94 us (3%)
    reduce_scatter x1, waiting for transfers between devices, on_device(): lax.psum_scatter(lax.dot_general(weight_rows, gated, (((0,), (1,)), ((),...  77.3 us
    all_gather x1, waiting for transfers between devices, on_device(): weight_rows = lax.all_gather(out_weight, 'seq', axis=1, tiled=True)  55.2 us
    all_to_all x2, blocking collectives, token_major(): return lax.all_to_all(block, 'seq', split_axis=1, concat_axis=0, tiled=True)  30.7 us
    all_to_all x1, waiting for transfers between devices, on_device(): lax.all_to_all(jnp.stack([cotangent] * lax.axis_size('chan')), 'chan', 0, 0)  23.5 us
    all_to_all x1, blocking collectives, channel_major(): return lax.all_to_all(block, 'seq', split_axis=0, concat_axis=1, tiled=True)  15.4 us
    all_to_all x1, waiting for transfers between devices, channel_major(): return lax.all_to_all(block, 'seq', split_axis=0, concat_axis=1, tiled=True)  10.4 us
    all_to_all x1, starting transfers between devices, on_device(): lax.all_to_all(jnp.stack([cotangent] * lax.axis_size('chan')), 'chan', 0, 0)  7.59 us
    dot_general x3, matrix products, forward_spectrum(): jnp.einsum('ckn,nm->ckm', turned_im, sin_second, precision=exact_mode)  6.78 us
  transfers between devices with their start and end apart: 6, of which 5 were waited for; matrix products, arithmetic and copies ran while one was open for 4% of the time, Pallas kernels for 0%

profile of v1, /device:TPU:2, one launch (start us, length us, event | category | flops | bytes accessed | tf_op | source)
XLA Modules:
  0.0 320.2 jit_solution(9123159588376874152)
XLA Ops:
  7.2 0.7 all-gather.2.cloned.1.call-update
  7.9 1.1 copy.51
  9.0 1.5 stack.10
  10.5 7.6 %all-to-all-start.2 = ((bf16[8,256,512]{1,2,0:T(8,128)(2,1)}), bf16[8,256,512]{1,2,0:T(8,128)(2,1)}, u32[]{:S(2)}, u32[]{:S(2)}) async-start(bf16[8,256,512]{1,2,0:T(8,128)(2,1)} %stack.10), calls=%async_computation.3 | async-start | bytes 4194304 | tf_op jit(solution)/shard_map/all_to_all | solution.py:143
  18.1 1.3 collective-permute-start
  19.8 0.4 convolution_negate_fusion
  20.2 0.4 fusion.68
  20.7 0.5 fusion.50
  21.5 0.5 fusion.3
  22.0 23.5 %all-to-all-done.2 = bf16[8,256,512]{1,2,0:T(8,128)(2,1)} async-done(((bf16[8,256,512]{1,2,0:T(8,128)(2,1)}), bf16[8,256,512]{1,2,0:T(8,128)(2,1)}, u32[]{:S(2)}, u32[]{:S(2)}) %all-to-all-start.2) | async-done | bytes 2097184 | tf_op jit(solution)/shard_map/all_to_all | solution.py:143
  45.5 55.2 %all-gather.2.cloned.1.call-done = bf16[512,4096]{1,0:T(8,128)(2,1)} async-done(((bf16[512,128]{1,0:T(8,128)(2,1)}), bf16[512,4096]{1,0:T(8,128)(2,1)}) %all-gather.2.cloned.1.call-update) | async-done | bytes 4194320 | tf_op jit(solution)/shard_map/all_gather | solution.py:133
  100.7 4.9 %multiply_convert_fusion = (bf16[256,512]{1,0:T(8,128)(2,1)S(1)}, f32[256,512]{1,0:T(8,128)}) fusion(f32[256,3,512]{2,0,1:T(8,128)S(1)} %fusion.3, bf16[256,4096]{0,1:T(8,128)(2,1)} %bitcast.27, bf16[512,4096]{1,0:T(8,128)(2,1)} %all-gather.2.cloned.1.call-done), kind=kOutput, calls=%fused_computation.89 | convolution fusion | flops 1074003968 | bytes 7602176 | tf_op jit(solution)/shard_map/dot_general | solution.py:145
  105.6 0.8 copy.52
  106.5 5.4 %all-to-all-start.3 = ((bf16[32,16,256]{2,1,0:T(8,128)(2,1)}), bf16[32,16,256]{2,1,0:T(8,128)(2,1)S(1)}, u32[]{:S(2)}, u32[]{:S(2)}) async-start(bf16[32,16,256]{2,1,0:T(8,128)(2,1)} %bitcast.30), calls=%async_computation.4 | async-start | bytes 524288 | tf_op jit(solution)/shard_map/all_to_all | solution.py:100
  112.1 0.5 fusion.54
  112.8 0.5 convolution_subtract_fusion.7
  113.3 0.5 convolution_add_fusion.9
  113.9 10.4 %all-to-all-done.3 = bf16[32,16,256]{2,1,0:T(8,128)(2,1)S(1)} async-done(((bf16[32,16,256]{2,1,0:T(8,128)(2,1)}), bf16[32,16,256]{2,1,0:T(8,128)(2,1)S(1)}, u32[]{:S(2)}, u32[]{:S(2)}) %all-to-all-start.3) | async-done | bytes 262176 | tf_op jit(solution)/shard_map/all_to_all | solution.py:100
  124.8 0.4 fusion.161
  125.3 0.4 fusion.6
  125.7 0.4 fusion.7
  126.1 2.1 fusion.48
  128.2 2.1 fusion.47
  130.3 2.1 convolution_subtract_fusion.1
  132.4 3.1 fusion.21
  135.5 1.6 fusion.88
  137.1 1.3 fusion.86
  138.4 1.4 convolution_subtract_fusion
  139.8 1.3 convolution_add_fusion
  141.1 1.5 fusion.26
  142.6 1.5 fusion.15
  144.4 15.3 %all_to_all.57 = bf16[16,32,256]{2,0,1:T(8,128)(2,1)S(1)} all-to-all(bf16[16,32,256]{2,0,1:T(8,128)(2,1)S(1)} %copy.64), channel_id=1, replica_groups=mesh['seq'=32,'chan'=8] {'seq'}, dimensions={1} | all-to-all | bytes 524288 | tf_op jit(solution)/shard_map/all_to_all | solution.py:104
  160.0 1.4 multiply_bitcast_fusion.1
  161.6 15.4 %all_to_all.58 = bf16[32,16,256]{2,1,0:T(8,128)(2,1)S(1)} all-to-all(bf16[32,16,256]{2,1,0:T(8,128)(2,1)S(1)} %bitcast.246), channel_id=1, replica_groups=mesh['seq'=32,'chan'=8] {'seq'}, dimensions={0} | all-to-all | bytes 524288 | tf_op jit(solution)/shard_map/all_to_all | solution.py:100
  177.6 0.4 fusion.163
  178.0 0.4 fusion.9
  178.4 0.4 fusion.10
  178.9 2.1 fusion.46
  180.9 2.1 fusion.45
  183.0 2.1 convolution_subtract_fusion.3
  185.1 3.1 fusion.19
  188.2 1.3 fusion.94
  189.6 1.5 fusion.92
  191.1 1.4 convolution_subtract_fusion.2
  192.5 1.3 convolution_add_fusion.2
  193.8 1.5 fusion.33
  195.3 2.2 fusion.16
  197.6 1.8 convert_element_type.266
  199.3 1.1 copy.49
  200.4 15.4 %all_to_all.59 = bf16[16,32,256]{2,0,1:T(8,128)(2,1)S(1)} all-to-all(bf16[16,32,256]{2,0,1:T(8,128)(2,1)S(1)} %copy.49), channel_id=1, replica_groups=mesh['seq'=32,'chan'=8] {'seq'}, dimensions={1} | all-to-all | bytes 524288 | tf_op jit(solution)/shard_map/all_to_all | solution.py:104
  215.8 0.9 convert_element_type.289
  216.7 2.1 copy.50
  218.7 5.8 %convolution_bitcast_fusion = f32[4096,256]{0,1:T(8,128)} fusion(bf16[512,4096]{1,0:T(8,128)(2,1)} %all-gather.2.cloned.1.call-done, f32[256,3,512]{2,0,1:T(8,128)} %copy-done, bf16[256,512]{1,0:T(8,128)(2,1)S(1)} %get-tuple-element.11, f32[512,256]{0,1:T(8,128)} %copy.50, f32[512]{0:T(512)S(1)} %copy-done.16), kind=kOutput, calls=%fused_computation | convolution fusion | flops 1074397184 | bytes 9701376 | tf_op jit(solution)/shard_map/dot_general | solution.py:135
  224.6 2.1 bitcast_reduce_fusion.1
  226.7 0.5 fusion.84
  227.2 0.5 fusion.82
  227.7 0.5 convolution_subtract_fusion.6
  228.2 0.5 convolution_add_fusion.8
  229.4 1.3 collective-permute-start.1
  231.1 0.7 copy.103
  231.8 0.7 collective-permute-done.1
  232.7 1.4 fusion.2
  234.1 77.3 %reduce-scatter.2.cloned.1.call-done = f32[512,256]{0,1:T(8,128)} async-done(((f32[4096,256]{0,1:T(8,128)}), f32[512,256]{0,1:T(8,128)}) %reduce-scatter.2.cloned.1.call-update) | async-done | bytes 524304 | tf_op jit(solution)/shard_map/reduce_scatter | solution.py:134
  311.4 1.8 convert_bitcast_fusion
  (67 shorter events, 4.0 us)
Async XLA Ops:
  7.2 93.5 %all-gather.2.cloned.1.call-start = ((), (), s32[]{:S(2)}) async-start(), calls=%async_computation.6 | async-start | bytes 4325376 | tf_op jit(solution)/shard_map/all_gather | solution.py:133
  10.5 7.6 %copy-start.10 = (bf16[256,3,512]{2,0,1:T(8,128)(2,1)S(1)}, bf16[256,3,512]{2,0,1:T(8,128)(2,1)}, u32[]{:S(2)}) copy-start(bf16[256,3,512]{2,0,1:T(8,128)(2,1)} %param.6) | copy-start | bytes 2359300
  10.5 9.2 %copy-start.18 = (f32[3,3,512]{2,1,0:T(4,128)S(1)}, f32[3,3,512]{2,1,0:T(4,128)}, u32[]{:S(2)}) copy-start(f32[3,3,512]{2,1,0:T(4,128)} %param.7) | copy-start | bytes 55300
  10.5 9.2 %copy-start.12 = (f32[2,8192]{1,0:T(2,128)S(1)}, f32[2,8192]{1,0:T(2,128)}, u32[]{:S(2)}) copy-start(f32[2,8192]{1,0:T(2,128)} %param.8) | copy-start | bytes 196612
  10.5 35.0 %all-to-all-start.2 = ((bf16[8,256,512]{1,2,0:T(8,128)(2,1)}), bf16[8,256,512]{1,2,0:T(8,128)(2,1)}, u32[]{:S(2)}, u32[]{:S(2)}) async-start(bf16[8,256,512]{1,2,0:T(8,128)(2,1)} %stack.10), calls=%async_computation.3 | async-start | bytes 4194304 | tf_op jit(solution)/shard_map/all_to_all | solution.py:143
  18.1 3.1 collective-permute-start
  19.7 93.6 %copy-start.2 = (f32[128,128]{1,0:T(8,128)}, f32[128,128]{1,0:T(8,128)S(1)}, u32[]{:S(2)}) copy-start(f32[128,128]{1,0:T(8,128)S(1)} %get-tuple-element.21) | copy-start | bytes 196612
  19.7 93.6 %copy-start.4 = (f32[128,128]{1,0:T(8,128)}, f32[128,128]{1,0:T(8,128)S(1)}, u32[]{:S(2)}) copy-start(f32[128,128]{1,0:T(8,128)S(1)} %get-tuple-element.22) | copy-start | bytes 196612
  21.2 0.7 copy-start.13
  22.0 83.6 %copy-start = (f32[256,3,512]{2,0,1:T(8,128)}, f32[256,3,512]{2,0,1:T(8,128)S(1)}, u32[]{:S(2)}) copy-start(f32[256,3,512]{2,0,1:T(8,128)S(1)} %fusion.3) | copy-start | bytes 4718596
  106.5 17.8 %all-to-all-start.3 = ((bf16[32,16,256]{2,1,0:T(8,128)(2,1)}), bf16[32,16,256]{2,1,0:T(8,128)(2,1)S(1)}, u32[]{:S(2)}, u32[]{:S(2)}) async-start(bf16[32,16,256]{2,1,0:T(8,128)(2,1)} %bitcast.30), calls=%async_computation.4 | async-start | bytes 524288 | tf_op jit(solution)/shard_map/all_to_all | solution.py:100
  111.8 199.5 %reduce-scatter.2.cloned.1.call-start = ((), (), s32[]{:S(2)}) async-start(), calls=%async_computation.7 | async-start | bytes 4718592 | tf_op jit(solution)/shard_map/reduce_scatter | solution.py:134
  113.3 19.0 %copy-start.6 = (f32[2,128,128]{2,1,0:T(8,128)}, f32[2,128,128]{2,1,0:T(8,128)S(1)}, u32[]{:S(2)}) copy-start(f32[2,128,128]{2,1,0:T(8,128)S(1)} %convolution_subtract_fusion.7) | copy-start | bytes 393220
  113.8 18.5 %copy-start.8 = (f32[2,128,128]{2,1,0:T(8,128)}, f32[2,128,128]{2,1,0:T(8,128)S(1)}, u32[]{:S(2)}) copy-start(f32[2,128,128]{2,1,0:T(8,128)S(1)} %convolution_add_fusion.9) | copy-start | bytes 393220
  144.2 15.8 %copy-start.15 = (f32[512]{0:T(512)S(1)}, f32[512]{0:T(512)}, u32[]{:S(2)}) copy-start(f32[512]{0:T(512)} %param.9) | copy-start | bytes 6148
  183.0 2.1 copy-start.7
  183.0 2.1 copy-start.9
  199.3 19.4 %copy-start.16 = (f32[512]{0:T(512)S(1)}, f32[512]{0:T(512)}, u32[]{:S(2)}) copy-start(f32[512]{0:T(512)} %param.9) | copy-start | bytes 6148
  224.6 4.2 %copy-start.3 = (f32[128,128]{1,0:T(8,128)S(1)}, f32[128,128]{1,0:T(8,128)}, u32[]{:S(2)}) copy-start(f32[128,128]{1,0:T(8,128)} %copy-done.2) | copy-start | bytes 196612
  224.6 4.2 %copy-start.5 = (f32[128,128]{1,0:T(8,128)S(1)}, f32[128,128]{1,0:T(8,128)}, u32[]{:S(2)}) copy-start(f32[128,128]{1,0:T(8,128)} %copy-done.4) | copy-start | bytes 196612
  226.6 2.5 copy-start.1
  226.6 2.5 copy-start.11
  226.7 2.5 copy-start.17
  229.4 3.1 collective-permute-start.1
  231.8 0.9 copy-start.14
Sparse Core Ops, SparseCore 0:
  9.7 90.9 all-gather.1
  224.7 86.6 reduce-scatter.1
